TPU v7x, 256 devices: a whole 4x4x8 slice. The times are simulated.
256 devices in a mesh: user: 8 (over x, core), item: 32 (over y, z).
Axes of the slice: x: 4, y: 4, z: 8, core: 2. Of those that a mesh axis runs over, the one named last changes fastest.
Arguments:
- user_factors: float32 [65536, 256], P(('user', 'item')), may hold values from -6 to 6
- item_factors: bfloat16 [131072, 256], P('item')
- head_ids: int32 [8], replicated, may hold values from 0 to 511, as said below
- tail_ids: int32 [256, 16], P(('user', 'item')), may hold values from 0 to 511, as said below
- head_counts: int32 [256, 8, 256, 256], P(('user', 'item')), may hold values from 0 to 7
- tail_counts: int32 [256, 16, 256, 256], P(('user', 'item')), may hold values from 0 to 7
Outputs:
- new_factors: float32 [65536, 256], P(('user', 'item'))
- residual: float32 [65536, 256], P(('user', 'item'))
Inputs may be any that keep to these rules, and one draw needn't show every extreme that they name: `head_ids`: 8 distinct block numbers, among them 0 and 511. `tail_ids`: each row holds distinct block numbers; at most 1 of a row fall in the range of one index of item (blocks o * 16 to (o + 1) * 16 - 1), and one range, the same for every row, holds exactly 1 of every row.
All inputs are finite; a program needn't handle non-finite values.
Results may differ from a plain program's by a relative error of at most 0.0055.
Values may be sent and summed in bfloat16 or wider, within the bound.
No kernel may reach another device: no remote copies, remote signals or barrier semaphores. Data moves between devices by JAX's collectives and lax.ppermute only.
A program may use at most 128 MiB of HBM per device.

v0:
```python
import jax
import jax.numpy as jnp
from jax import lax
from jax.sharding import PartitionSpec as P

ITERS = 2
conf_alpha = 4.0
ridge_term = 0.1
epsilon = 1e-06


def broadcast(shard, axis, root):
    mine = lax.axis_index(axis) == root
    return lax.psum(jnp.where(mine, shard, jnp.zeros_like(shard)), axis)


def apply_operator(vector, gram_matrix, item_tiles, weights):
    rounded = vector.astype(jnp.bfloat16)
    scores = jnp.einsum("uf,kif->kui", rounded, item_tiles, preferred_element_type=jnp.float32)
    scaled = (scores * weights).astype(jnp.bfloat16)
    data_term = jnp.einsum("kui,kif->uf", scaled, item_tiles, preferred_element_type=jnp.float32)
    gram_term = jnp.dot(vector, gram_matrix, precision=lax.Precision.HIGHEST)
    return gram_term + ridge_term * vector + data_term


def solve_block(start_vec, gram_matrix, item_tiles, counts):
    count_float = counts.astype(jnp.float32)
    weights = (conf_alpha * count_float).astype(jnp.bfloat16)
    rated_weight = jnp.where(counts > 0, 1.0 + conf_alpha * count_float, 0.0).astype(jnp.bfloat16)
    rhs = jnp.einsum("kui,kif->uf", rated_weight, item_tiles, preferred_element_type=jnp.float32)
    solution = start_vec
    residual = rhs - apply_operator(solution, gram_matrix, item_tiles, weights)
    direction = residual
    norm_now = jnp.sum(residual * residual, axis=1, keepdims=True)
    for turn_index in range(ITERS):
        image_vec = apply_operator(direction, gram_matrix, item_tiles, weights)
        step_size = norm_now / (jnp.sum(direction * image_vec, axis=1, keepdims=True) + epsilon)
        solution = solution + step_size * direction
        residual = residual - step_size * image_vec
        if turn_index + 1 < ITERS:
            norm_next = jnp.sum(residual * residual, axis=1, keepdims=True)
            direction = residual + norm_next / (norm_now + epsilon) * direction
            norm_now = norm_next
    return (solution, residual)


def local(user_factors, item_factors, head_ids, tail_ids, head_counts, tail_counts):
    item_count = lax.axis_size("item")
    user_count = lax.axis_size("user")
    block_size = head_counts.shape[-1]
    rank_width = item_factors.shape[1]
    shard_blocks = item_factors.shape[0] // block_size
    blocks = item_factors.reshape(shard_blocks, block_size, rank_width)
    contract = (((0,), (0,)), ((), ()))
    slice_rows = item_factors.shape[0] // user_count
    rows_part = lax.dynamic_slice_in_dim(
        item_factors, lax.axis_index("user") * slice_rows, slice_rows, 0
    )
    local_gram = lax.dot_general(rows_part, rows_part, contract, preferred_element_type=jnp.float32)
    gram_matrix = lax.psum(local_gram, ("user", "item"))
    head_owner = head_ids // shard_blocks
    head_local = head_ids % shard_blocks
    head_total = head_ids.shape[0]

    def take_turn(index, gathered):
        block_rows = lax.dynamic_index_in_dim(blocks, head_local[index], 0, keepdims=False)
        arrived = broadcast(block_rows, "item", head_owner[index])
        return lax.dynamic_update_index_in_dim(gathered, arrived, index, 0)

    empty = jnp.zeros((head_total, block_size, rank_width), jnp.bfloat16)
    head_rows = lax.fori_loop(0, head_total, take_turn, empty)
    wanted = tail_ids.reshape(-1)
    length = wanted.shape[0]
    capacity = 2 * length // item_count
    owner_of = wanted // shard_blocks
    local_of = wanted % shard_blocks
    same_owner = owner_of[:, None] == owner_of[None, :]
    positions = jnp.arange(length, dtype=jnp.int32)
    earlier = positions[:, None] > positions[None, :]
    place_index = jnp.sum((same_owner & earlier).astype(jnp.int32), axis=1)
    slot_index = owner_of * capacity + place_index
    slot_table = slot_index[:, None] == jnp.arange(item_count * capacity, dtype=jnp.int32)[None, :]
    requests = jnp.sum(jnp.where(slot_table, local_of[:, None], 0), axis=0)
    requests = requests.reshape(item_count, capacity)
    served = blocks[lax.all_to_all(requests, "item", split_axis=0, concat_axis=0, tiled=True)]
    arrived_tail = lax.all_to_all(served, "item", split_axis=0, concat_axis=0, tiled=True)
    tail_rows = arrived_tail.reshape(item_count * capacity, block_size, rank_width)[slot_index]
    local_blocks = tail_ids.shape[0]
    tail_tiles = tail_rows.reshape(local_blocks, tail_ids.shape[1], block_size, rank_width)
    start_blocks = user_factors.reshape(local_blocks, block_size, rank_width)

    def one_block(block_args):
        start_vec, tail_part_rows, head_part, tail_part = block_args
        item_tiles = jnp.concatenate([head_rows, tail_part_rows], axis=0)
        counts = jnp.concatenate([head_part, tail_part], axis=0)
        return solve_block(start_vec, gram_matrix, item_tiles, counts)

    solution, residual = lax.map(one_block, (start_blocks, tail_tiles, head_counts, tail_counts))
    return (
        solution.reshape(local_blocks * block_size, rank_width),
        residual.reshape(local_blocks * block_size, rank_width),
    )


def solution(mesh):
    return jax.shard_map(
        local,
        mesh=mesh,
        in_specs=(
            P(("user", "item"), None),
            P("item", None),
            P(),
            P(("user", "item"), None),
            P(("user", "item"), None, None, None),
            P(("user", "item"), None, None, None),
        ),
        out_specs=(P(("user", "item"), None), P(("user", "item"), None)),
        check_vma=False,
    )
```

profile of v0, /device:TPU:2, one launch (start us, length us, event | category | flops | bytes accessed | tf_op | source)
XLA Modules:
  0.0 1522.7 jit_solution(15008813980043057980)
XLA Ops:
  9.7 21.1 %all_to_all.14 = s32[32,1,1]{2,1,0:T(1,128)S(1)} all-to-all(s32[32,1,1]{2,1,0:T(1,128)S(1)} %copy.57), channel_id=1, replica_groups=mesh['user'=8,'item'=32] {'item'}, dimensions={0} | all-to-all | bytes 256 | tf_op jit(solution)/shard_map/all_to_all | solution.py:85
  31.5 4.4 gather_fusion
  35.8 5.0 all-to-all-start.1
  40.9 2.0 fusion.32
  42.9 1194.5 %while.8 = (s32[]{:T(128)}, bf16[8,256,256]{1,2,0:T(8,128)(2,1)}, s32[8]{0:T(128)S(1)}, s32[8]{0:T(128)S(1)}, bf16[16,256,256]{2,1,0:T(8,128)(2,1)}, /*index=5*/s32[]{:T(128)}, s32[]{:T(128)}, s32[]{:T(128)}, u32[]{:T(128)}) while((s32[]{:T(128)}, bf16[8,256,256]{1,2,0:T(8,128)(2,1)}, s32[8]{0:T(128)S(1)}, s32[8]{0:T(128)S(1)}, ...), condition=%wide.region_2.3_spmd, body=%wide.region_0.2_spmd.sunk | while | flops 131080 | bytes 1573101 | solution.py:71
  46.6 1.6 dynamic-slice_select_fusion.2
  48.2 151.8 %all-reduce.5.cloned.1.call-done = bf16[1,256,256]{2,1,0:T(8,128)(2,1)} async-done(((bf16[1,256,256]{2,1,0:T(8,128)(2,1)}), bf16[1,256,256]{2,1,0:T(8,128)(2,1)}) %all-reduce.5.cloned.1.call-update) | async-done | bytes 131088 | tf_op jit(solution)/shard_map/while/body/eval_jaxpr/psum | solution.py:14
  200.0 1.0 copy.87
  205.3 1.6 dynamic-slice_select_fusion.2
  206.9 141.0 %all-reduce.5.cloned.1.call-done = bf16[1,256,256]{2,1,0:T(8,128)(2,1)} async-done(((bf16[1,256,256]{2,1,0:T(8,128)(2,1)}), bf16[1,256,256]{2,1,0:T(8,128)(2,1)}) %all-reduce.5.cloned.1.call-update) | async-done | bytes 131088 | tf_op jit(solution)/shard_map/while/body/eval_jaxpr/psum | solution.py:14
  353.3 1.6 dynamic-slice_select_fusion.2
  354.9 141.0 %all-reduce.5.cloned.1.call-done = bf16[1,256,256]{2,1,0:T(8,128)(2,1)} async-done(((bf16[1,256,256]{2,1,0:T(8,128)(2,1)}), bf16[1,256,256]{2,1,0:T(8,128)(2,1)}) %all-reduce.5.cloned.1.call-update) | async-done | bytes 131088 | tf_op jit(solution)/shard_map/while/body/eval_jaxpr/psum | solution.py:14
  501.2 1.6 dynamic-slice_select_fusion.2
  502.8 141.0 %all-reduce.5.cloned.1.call-done = bf16[1,256,256]{2,1,0:T(8,128)(2,1)} async-done(((bf16[1,256,256]{2,1,0:T(8,128)(2,1)}), bf16[1,256,256]{2,1,0:T(8,128)(2,1)}) %all-reduce.5.cloned.1.call-update) | async-done | bytes 131088 | tf_op jit(solution)/shard_map/while/body/eval_jaxpr/psum | solution.py:14
  649.2 1.6 dynamic-slice_select_fusion.2
  650.8 141.0 %all-reduce.5.cloned.1.call-done = bf16[1,256,256]{2,1,0:T(8,128)(2,1)} async-done(((bf16[1,256,256]{2,1,0:T(8,128)(2,1)}), bf16[1,256,256]{2,1,0:T(8,128)(2,1)}) %all-reduce.5.cloned.1.call-update) | async-done | bytes 131088 | tf_op jit(solution)/shard_map/while/body/eval_jaxpr/psum | solution.py:14
  797.1 1.6 dynamic-slice_select_fusion.2
  798.7 141.0 %all-reduce.5.cloned.1.call-done = bf16[1,256,256]{2,1,0:T(8,128)(2,1)} async-done(((bf16[1,256,256]{2,1,0:T(8,128)(2,1)}), bf16[1,256,256]{2,1,0:T(8,128)(2,1)}) %all-reduce.5.cloned.1.call-update) | async-done | bytes 131088 | tf_op jit(solution)/shard_map/while/body/eval_jaxpr/psum | solution.py:14
  945.1 1.6 dynamic-slice_select_fusion.2
  946.7 141.0 %all-reduce.5.cloned.1.call-done = bf16[1,256,256]{2,1,0:T(8,128)(2,1)} async-done(((bf16[1,256,256]{2,1,0:T(8,128)(2,1)}), bf16[1,256,256]{2,1,0:T(8,128)(2,1)}) %all-reduce.5.cloned.1.call-update) | async-done | bytes 131088 | tf_op jit(solution)/shard_map/while/body/eval_jaxpr/psum | solution.py:14
  1093.1 1.6 dynamic-slice_select_fusion.2
  1094.6 141.0 %all-reduce.5.cloned.1.call-done = bf16[1,256,256]{2,1,0:T(8,128)(2,1)} async-done(((bf16[1,256,256]{2,1,0:T(8,128)(2,1)}), bf16[1,256,256]{2,1,0:T(8,128)(2,1)}) %all-reduce.5.cloned.1.call-update) | async-done | bytes 131088 | tf_op jit(solution)/shard_map/while/body/eval_jaxpr/psum | solution.py:14
  1237.9 5.5 copy.56
  1243.4 1.9 copy.55
  1245.5 2.9 gather_fusion.1
  1248.3 2.4 copy.59
  1250.7 6.8 fusion.23
  1257.6 4.5 fusion.17
  1262.1 233.9 %all-reduce.3.cloned.1.call-done = f32[256,256]{1,0:T(8,128)} async-done(((f32[256,256]{1,0:T(8,128)}), f32[256,256]{1,0:T(8,128)}) %all-reduce.3.cloned.1.call-update) | async-done | bytes 262160 | tf_op jit(solution)/shard_map/psum | solution.py:60
  1496.0 1.5 fusion.22
  1497.6 7.6 fusion.26
  1506.0 6.9 fusion.29
  (87 shorter events, 27.9 us)
Async XLA Ops:
  35.8 7.0 copy-start.5
  35.8 1209.6 %all-to-all-start.1 = ((bf16[32,1,256,256]{3,2,1,0:T(8,128)(2,1)}), bf16[32,1,256,256]{3,2,1,0:T(8,128)(2,1)}, u32[]{:S(2)}, u32[]{:S(2)}) async-start(bf16[32,1,256,256]{3,2,1,0:T(8,128)(2,1)} %bitcast.94), calls=%async_computation.1 | async-start | bytes 8388608 | tf_op jit(solution)/shard_map/all_to_all | solution.py:86
  42.9 157.1 %all-reduce.5.cloned.1.call-start = ((), (), s32[]{:S(2)}) async-start(), calls=%async_computation.3 | async-start | bytes 262144 | tf_op jit(solution)/shard_map/while/body/eval_jaxpr/psum | solution.py:14
  201.7 146.3 %all-reduce.5.cloned.1.call-start = ((), (), s32[]{:S(2)}) async-start(), calls=%async_computation.3 | async-start | bytes 262144 | tf_op jit(solution)/shard_map/while/body/eval_jaxpr/psum | solution.py:14
  349.6 146.3 %all-reduce.5.cloned.1.call-start = ((), (), s32[]{:S(2)}) async-start(), calls=%async_computation.3 | async-start | bytes 262144 | tf_op jit(solution)/shard_map/while/body/eval_jaxpr/psum | solution.py:14
  497.6 146.3 %all-reduce.5.cloned.1.call-start = ((), (), s32[]{:S(2)}) async-start(), calls=%async_computation.3 | async-start | bytes 262144 | tf_op jit(solution)/shard_map/while/body/eval_jaxpr/psum | solution.py:14
  645.5 146.3 %all-reduce.5.cloned.1.call-start = ((), (), s32[]{:S(2)}) async-start(), calls=%async_computation.3 | async-start | bytes 262144 | tf_op jit(solution)/shard_map/while/body/eval_jaxpr/psum | solution.py:14
  793.5 146.3 %all-reduce.5.cloned.1.call-start = ((), (), s32[]{:S(2)}) async-start(), calls=%async_computation.3 | async-start | bytes 262144 | tf_op jit(solution)/shard_map/while/body/eval_jaxpr/psum | solution.py:14
  941.4 146.3 %all-reduce.5.cloned.1.call-start = ((), (), s32[]{:S(2)}) async-start(), calls=%async_computation.3 | async-start | bytes 262144 | tf_op jit(solution)/shard_map/while/body/eval_jaxpr/psum | solution.py:14
  1089.4 146.3 %all-reduce.5.cloned.1.call-start = ((), (), s32[]{:S(2)}) async-start(), calls=%async_computation.3 | async-start | bytes 262144 | tf_op jit(solution)/shard_map/while/body/eval_jaxpr/psum | solution.py:14
  1237.3 258.7 %all-reduce.3.cloned.1.call-start = ((), (), s32[]{:S(2)}) async-start(), calls=%async_computation.2 | async-start | bytes 524288 | tf_op jit(solution)/shard_map/psum | solution.py:60
  1237.9 5.5 copy-start.1
  1243.4 1.9 copy-start.3
  1243.4 2.0 copy-start.6
  1250.7 6.8 copy-start.2
  1497.6 7.6 copy-start
  1497.6 8.4 copy-start.4
Sparse Core Ops, SparseCore 0:
  48.3 151.6 all-reduce.4
  207.0 140.8 all-reduce.4
  355.0 140.8 all-reduce.4
  503.0 140.8 all-reduce.4
  650.9 140.8 all-reduce.4
  798.9 140.8 all-reduce.4
  946.8 140.8 all-reduce.4
  1094.8 140.8 all-reduce.4
Sparse Core Ops, SparseCore 1:
  1243.8 252.1 all-reduce.2
where the time goes:
time: 1520 us
  waiting for transfers between devices  1370 us (90%)
  local copies, waits for them, and re-layouts  41.4 us (3%)
  matrix products  30.6 us (2%)
  blocking collectives  21.1 us (1%)
  loops' own time  20.3 us (1%)
  between operations  15.7 us (1%)
    psum x8, waiting for transfers between devices, broadcast(): return lax.psum(jnp.where(mine, shard, jnp.zeros_like(shard)), axis)  1140 us
    psum x1, waiting for transfers between devices, local(): gram_matrix = lax.psum(local_gram, ('user', 'item'))  234 us
  transfers between devices with their start and end apart: 10, of which 9 were waited for; matrix products, arithmetic and copies ran while one was open for 4% of the time, Pallas kernels for 0%

commit v1 on v0

--- a/solution.py
+++ b/solution.py
@@ -57,7 +57,7 @@
         item_factors, lax.axis_index("user") * slice_rows, slice_rows, 0
     )
     local_gram = lax.dot_general(rows_part, rows_part, contract, preferred_element_type=jnp.float32)
-    gram_matrix = lax.psum(local_gram, ("user", "item"))
+    gram_matrix = lax.psum(lax.psum(local_gram, "item"), "user")
     head_owner = head_ids // shard_blocks
     head_local = head_ids % shard_blocks
     head_total = head_ids.shape[0]

time: 1520 us -> 1480 us (0.974)
  waiting for transfers between devices: 1370 us -> 1320 us
    psum x1 -> x2, waiting for transfers between devices: 234 us -> 185 us  [local(): gram_matrix = lax.psum(lax.psum(local_gram, 'item'), 'user')]
  transfers between devices with their start and end apart: 10 -> 11, of which waited for: 9 -> 10; matrix products, arithmetic and copies ran while one was open for 4% -> 4% of each run, Pallas kernels for 0% -> 0%
where the time goes in v1:
time: 1480 us; the launch traced here: 1470 us
  waiting for transfers between devices  1320 us (89%)
  local copies, waits for them, and re-layouts  41.4 us (3%)
  matrix products  30.5 us (2%)
  blocking collectives  21.1 us (1%)
  loops' own time  20.3 us (1%)
  between operations  15.7 us (1%)
  other arithmetic  15.1 us (1%)
    psum x8, waiting for transfers between devices, broadcast(): return lax.psum(jnp.where(mine, shard, jnp.zeros_like(shard)), axis)  1140 us
    psum x2, waiting for transfers between devices, local(): gram_matrix = lax.psum(lax.psum(local_gram, 'item'), 'user')  185 us
  transfers between devices with their start and end apart: 11, of which 10 were waited for; matrix products, arithmetic and copies ran while one was open for 4% of the time, Pallas kernels for 0%

profile of v1, /device:TPU:2, one launch (start us, length us, event | category | flops | bytes accessed | tf_op | source)
XLA Modules:
  0.0 1474.1 jit_solution(16898312211751599183)
XLA Ops:
  9.7 21.1 %all_to_all.14 = s32[32,1,1]{2,1,0:T(1,128)S(1)} all-to-all(s32[32,1,1]{2,1,0:T(1,128)S(1)} %copy.57), channel_id=1, replica_groups=mesh['user'=8,'item'=32] {'item'}, dimensions={0} | all-to-all | bytes 256 | tf_op jit(solution)/shard_map/all_to_all | solution.py:85
  31.5 4.4 gather_fusion
  35.8 5.0 all-to-all-start.1
  40.9 2.0 fusion.32
  42.9 1194.5 %while.8 = (s32[]{:T(128)}, bf16[8,256,256]{1,2,0:T(8,128)(2,1)}, s32[8]{0:T(128)S(1)}, s32[8]{0:T(128)S(1)}, bf16[16,256,256]{2,1,0:T(8,128)(2,1)}, /*index=5*/s32[]{:T(128)}, s32[]{:T(128)}, s32[]{:T(128)}, u32[]{:T(128)}) while((s32[]{:T(128)}, bf16[8,256,256]{1,2,0:T(8,128)(2,1)}, s32[8]{0:T(128)S(1)}, s32[8]{0:T(128)S(1)}, ...), condition=%wide.region_2.3_spmd, body=%wide.region_0.2_spmd.sunk | while | flops 131080 | bytes 1573101 | solution.py:71
  46.6 1.6 dynamic-slice_select_fusion.2
  48.2 151.8 %all-reduce.8.cloned.1.call-done = bf16[1,256,256]{2,1,0:T(8,128)(2,1)} async-done(((bf16[1,256,256]{2,1,0:T(8,128)(2,1)}), bf16[1,256,256]{2,1,0:T(8,128)(2,1)}) %all-reduce.8.cloned.1.call-update) | async-done | bytes 131088 | tf_op jit(solution)/shard_map/while/body/eval_jaxpr/psum | solution.py:14
  205.3 1.6 dynamic-slice_select_fusion.2
  206.9 141.0 %all-reduce.8.cloned.1.call-done = bf16[1,256,256]{2,1,0:T(8,128)(2,1)} async-done(((bf16[1,256,256]{2,1,0:T(8,128)(2,1)}), bf16[1,256,256]{2,1,0:T(8,128)(2,1)}) %all-reduce.8.cloned.1.call-update) | async-done | bytes 131088 | tf_op jit(solution)/shard_map/while/body/eval_jaxpr/psum | solution.py:14
  353.3 1.6 dynamic-slice_select_fusion.2
  354.9 141.0 %all-reduce.8.cloned.1.call-done = bf16[1,256,256]{2,1,0:T(8,128)(2,1)} async-done(((bf16[1,256,256]{2,1,0:T(8,128)(2,1)}), bf16[1,256,256]{2,1,0:T(8,128)(2,1)}) %all-reduce.8.cloned.1.call-update) | async-done | bytes 131088 | tf_op jit(solution)/shard_map/while/body/eval_jaxpr/psum | solution.py:14
  501.2 1.6 dynamic-slice_select_fusion.2
  502.8 141.0 %all-reduce.8.cloned.1.call-done = bf16[1,256,256]{2,1,0:T(8,128)(2,1)} async-done(((bf16[1,256,256]{2,1,0:T(8,128)(2,1)}), bf16[1,256,256]{2,1,0:T(8,128)(2,1)}) %all-reduce.8.cloned.1.call-update) | async-done | bytes 131088 | tf_op jit(solution)/shard_map/while/body/eval_jaxpr/psum | solution.py:14
  649.2 1.6 dynamic-slice_select_fusion.2
  650.8 141.0 %all-reduce.8.cloned.1.call-done = bf16[1,256,256]{2,1,0:T(8,128)(2,1)} async-done(((bf16[1,256,256]{2,1,0:T(8,128)(2,1)}), bf16[1,256,256]{2,1,0:T(8,128)(2,1)}) %all-reduce.8.cloned.1.call-update) | async-done | bytes 131088 | tf_op jit(solution)/shard_map/while/body/eval_jaxpr/psum | solution.py:14
  797.1 1.6 dynamic-slice_select_fusion.2
  798.7 141.0 %all-reduce.8.cloned.1.call-done = bf16[1,256,256]{2,1,0:T(8,128)(2,1)} async-done(((bf16[1,256,256]{2,1,0:T(8,128)(2,1)}), bf16[1,256,256]{2,1,0:T(8,128)(2,1)}) %all-reduce.8.cloned.1.call-update) | async-done | bytes 131088 | tf_op jit(solution)/shard_map/while/body/eval_jaxpr/psum | solution.py:14
  945.1 1.6 dynamic-slice_select_fusion.2
  946.7 141.0 %all-reduce.8.cloned.1.call-done = bf16[1,256,256]{2,1,0:T(8,128)(2,1)} async-done(((bf16[1,256,256]{2,1,0:T(8,128)(2,1)}), bf16[1,256,256]{2,1,0:T(8,128)(2,1)}) %all-reduce.8.cloned.1.call-update) | async-done | bytes 131088 | tf_op jit(solution)/shard_map/while/body/eval_jaxpr/psum | solution.py:14
  1093.1 1.6 dynamic-slice_select_fusion.2
  1094.6 141.0 %all-reduce.8.cloned.1.call-done = bf16[1,256,256]{2,1,0:T(8,128)(2,1)} async-done(((bf16[1,256,256]{2,1,0:T(8,128)(2,1)}), bf16[1,256,256]{2,1,0:T(8,128)(2,1)}) %all-reduce.8.cloned.1.call-update) | async-done | bytes 131088 | tf_op jit(solution)/shard_map/while/body/eval_jaxpr/psum | solution.py:14
  1238.1 5.5 copy.56
  1243.6 1.9 copy.55
  1245.7 139.7 %all-reduce.4.cloned.1.call-done = f32[256,256]{1,0:T(8,128)} async-done(((f32[256,256]{1,0:T(8,128)}), f32[256,256]{1,0:T(8,128)}) %all-reduce.4.cloned.1.call-update) | async-done | bytes 262160 | tf_op jit(solution)/shard_map/psum | solution.py:60
  1385.4 2.9 gather_fusion.1
  1388.2 2.4 copy.59
  1390.6 6.8 fusion.23
  1397.5 4.5 fusion.17
  1402.0 45.5 %all-reduce.6.cloned.1.call-done = f32[256,256]{1,0:T(8,128)} async-done(((f32[256,256]{1,0:T(8,128)}), f32[256,256]{1,0:T(8,128)}) %all-reduce.6.cloned.1.call-update) | async-done | bytes 262160 | tf_op jit(solution)/shard_map/psum | solution.py:60
  1447.4 1.5 fusion.22
  1449.0 7.6 fusion.26
  1457.4 6.9 fusion.29
  (90 shorter events, 29.1 us)
Async XLA Ops:
  35.8 7.0 copy-start.5
  35.8 1349.5 %all-to-all-start.1 = ((bf16[32,1,256,256]{3,2,1,0:T(8,128)(2,1)}), bf16[32,1,256,256]{3,2,1,0:T(8,128)(2,1)}, u32[]{:S(2)}, u32[]{:S(2)}) async-start(bf16[32,1,256,256]{3,2,1,0:T(8,128)(2,1)} %bitcast.94), calls=%async_computation.1 | async-start | bytes 8388608 | tf_op jit(solution)/shard_map/all_to_all | solution.py:86
  42.9 157.1 %all-reduce.8.cloned.1.call-start = ((), (), s32[]{:S(2)}) async-start(), calls=%async_computation.4 | async-start | bytes 262144 | tf_op jit(solution)/shard_map/while/body/eval_jaxpr/psum | solution.py:14
  201.7 146.3 %all-reduce.8.cloned.1.call-start = ((), (), s32[]{:S(2)}) async-start(), calls=%async_computation.4 | async-start | bytes 262144 | tf_op jit(solution)/shard_map/while/body/eval_jaxpr/psum | solution.py:14
  349.6 146.3 %all-reduce.8.cloned.1.call-start = ((), (), s32[]{:S(2)}) async-start(), calls=%async_computation.4 | async-start | bytes 262144 | tf_op jit(solution)/shard_map/while/body/eval_jaxpr/psum | solution.py:14
  497.6 146.3 %all-reduce.8.cloned.1.call-start = ((), (), s32[]{:S(2)}) async-start(), calls=%async_computation.4 | async-start | bytes 262144 | tf_op jit(solution)/shard_map/while/body/eval_jaxpr/psum | solution.py:14
  645.5 146.3 %all-reduce.8.cloned.1.call-start = ((), (), s32[]{:S(2)}) async-start(), calls=%async_computation.4 | async-start | bytes 262144 | tf_op jit(solution)/shard_map/while/body/eval_jaxpr/psum | solution.py:14
  793.5 146.3 %all-reduce.8.cloned.1.call-start = ((), (), s32[]{:S(2)}) async-start(), calls=%async_computation.4 | async-start | bytes 262144 | tf_op jit(solution)/shard_map/while/body/eval_jaxpr/psum | solution.py:14
  941.4 146.3 %all-reduce.8.cloned.1.call-start = ((), (), s32[]{:S(2)}) async-start(), calls=%async_computation.4 | async-start | bytes 262144 | tf_op jit(solution)/shard_map/while/body/eval_jaxpr/psum | solution.py:14
  1089.4 146.3 %all-reduce.8.cloned.1.call-start = ((), (), s32[]{:S(2)}) async-start(), calls=%async_computation.4 | async-start | bytes 262144 | tf_op jit(solution)/shard_map/while/body/eval_jaxpr/psum | solution.py:14
  1237.3 148.0 %all-reduce.4.cloned.1.call-start = ((), (), s32[]{:S(2)}) async-start(), calls=%async_computation.2 | async-start | bytes 524288 | tf_op jit(solution)/shard_map/psum | solution.py:60
  1237.9 5.7 copy-start.1
  1237.9 209.5 %all-reduce.6.cloned.1.call-start = ((), (), s32[]{:S(2)}) async-start(), calls=%async_computation.3 | async-start | bytes 524288 | tf_op jit(solution)/shard_map/psum | solution.py:60
  1243.6 1.9 copy-start.3
  1243.6 2.0 copy-start.6
  1390.6 6.8 copy-start.2
  1449.0 7.6 copy-start
  1449.0 8.4 copy-start.4
Sparse Core Ops, SparseCore 0:
  48.3 151.6 all-reduce.7
  207.0 140.8 all-reduce.7
  355.0 140.8 all-reduce.7
  503.0 140.8 all-reduce.7
  650.9 140.8 all-reduce.7
  798.9 140.8 all-reduce.7
  946.8 140.8 all-reduce.7
  1094.8 140.8 all-reduce.7
Sparse Core Ops, SparseCore 1:
  1241.8 143.4 all-reduce.3
  1387.5 59.8 all-reduce.5
